TPU v7x, 32 devices: a whole 2x2x4 slice. The times are simulated.
32 devices in a mesh: view: 2 (over y), tile: 4 (over z), slab: 4 (over x, core).
Axes of the slice: x: 2, y: 2, z: 4, core: 2. Of those that a mesh axis runs over, the one named last changes fastest.
Arguments:
- estimate: float32 [64, 64, 128], P('slab', 'tile'), may hold values from 0.5 to 2
- recorded: float32 [2, 64, 64, 128], P('view', 'slab', 'tile'), may hold values from 0.25 to 4
- x_index: int32 [2, 64, 128], P('view', 'slab'), may hold values from 0 to 15
- y_index: int32 [2, 64, 64], P('view', 'slab', 'tile'), may hold values from 0 to 15
- z_index: int32 [2, 64, 128], P('view', 'tile'), may hold values from 0 to 15
- profiles: float32 [2, 3, 16, 31], P('view'), may hold values from 0.01 to 1
Outputs:
- updated: float32 [64, 64, 128], P('slab', 'tile')
All inputs are finite; a program needn't handle non-finite values.
Results may differ from a plain program's by a relative error of at most 0.00005.
Values sent between devices are 32-bit elements; how exact they have to be, the bound alone decides.
A program may use at most 64 MiB of HBM per device.

v0:
```python
import jax
import jax.numpy as jnp
from jax import lax
from jax.sharding import PartitionSpec as P


def with_halo(shard, sides, width):
    for axis, dim in sides:
        devices, length = (lax.axis_size(axis), shard.shape[dim])
        up = [(i, (i + 1) % devices) for i in range(devices - 1)]
        down = [(j, i) for i, j in up]
        last = lax.slice_in_dim(shard, length - width, length, axis=dim)
        initial = lax.slice_in_dim(shard, 0, width, axis=dim)
        before = lax.ppermute(last, axis, up)
        after = lax.ppermute(initial, axis, down)
        shard = jnp.concatenate([before, shard, after], axis=dim)
    return shard


def banded(padded, weights, dim, adjoint):
    count = padded.shape[dim] - 30
    total = None
    for k in range(31):
        start = 30 - k if adjoint else k
        term = weights[..., k] * lax.slice_in_dim(padded, start, start + count, axis=dim)
        total = term if total is None else total + term
    return total


def pad_along(field, dim):
    widths = [(0, 0)] * field.ndim
    widths[dim] = (15, 15)
    return jnp.pad(field, widths)


def lookup(index_map, table):
    levels = jnp.arange(table.shape[1], dtype=jnp.int32)
    onehot = (index_map[..., None] == levels).astype(jnp.float32)
    return jnp.einsum("vabp,vpk->vabk", onehot, table, precision=lax.Precision.HIGHEST)


def z_blur(field, z_taps, adjoint):
    margin = with_halo(field, (("slab", 1),), 15)
    return banded(margin, z_taps[:, None], 1, adjoint)


def shards(estimate, recorded, x_index, y_index, z_index, profiles):
    views_here = recorded.shape[0]
    weights = profiles / jnp.sum(profiles, axis=-1, keepdims=True)
    x_taps = lookup(x_index, weights[:, 0])[:, :, None, :, :]
    y_taps = lookup(y_index, weights[:, 1])[:, :, :, None, :]
    z_taps = lookup(z_index, weights[:, 2])
    widened = with_halo(estimate, (("tile", 1),), 15)
    along_x = banded(widened, x_taps, 1, False)
    along_y = banded(pad_along(along_x, 3), y_taps, 3, False)
    blurred = z_blur(along_y, z_taps, False)
    ratio = recorded / blurred
    back_z = z_blur(ratio, z_taps, True)
    back_y = banded(pad_along(back_z, 3), y_taps, 3, True)
    margin = with_halo(back_y, (("tile", 2),), 15)
    back_x = banded(margin, x_taps, 2, True)
    local_sum = jnp.sum(back_x, axis=0)
    total = lax.psum(local_sum, "view")
    return estimate * total / (views_here * lax.axis_size("view"))


def solution(mesh):
    placed = (
        P("slab", "tile", None),
        P("view", "slab", "tile", None),
        P("view", "slab", None),
        P("view", "slab", "tile"),
        P("view", "tile", None),
        P("view", None, None, None),
    )
    return jax.shard_map(
        shards, mesh=mesh, in_specs=placed, out_specs=P("slab", "tile", None), check_vma=False
    )
```

profile of v0, /device:TPU:0, one launch (start us, length us, event | category | flops | bytes accessed | tf_op | source)
XLA Modules:
  0.0 85.9 jit_solution(4088150595432847791)
XLA Ops:
  6.5 1.0 %fusion.455 = (f32[16,15,128]{2,1,0:T(8,128)S(1)}, f32[16,15,128]{2,1,0:T(8,128)S(1)}) fusion(f32[16,16,128]{2,1,0:T(8,128)} %param.6), kind=kLoop, calls=%fused_computation.777 | loop fusion | bytes 491520 | tf_op jit(solution)/shard_map/slice | solution.py:13
  7.5 1.3 %collective-permute-start.1 = (f32[16,15,128]{2,1,0:T(8,128)S(1)}, f32[16,15,128]{2,1,0:T(8,128)S(1)}, u32[]{:S(2)}, u32[]{:S(2)}) collective-permute-start(f32[16,15,128]{2,1,0:T(8,128)S(1)} %get-tuple-element.104), channel_id=1, source_target_pairs={{4,0},{8,4},{12,8},{5,1},{9,5},{13,9},{6,2},{10,6},{14,10},{7,3},{... | collective-permute-start | bytes 368648 | tf_op jit(solution)/shard_map/ppermute | solution.py:15
  8.8 5.6 %collective-permute-start = (f32[16,15,128]{2,1,0:T(8,128)S(1)}, f32[16,15,128]{2,1,0:T(8,128)S(1)}, u32[]{:S(2)}, u32[]{:S(2)}) collective-permute-start(f32[16,15,128]{2,1,0:T(8,128)S(1)} %get-tuple-element.105), channel_id=1, source_target_pairs={{0,4},{4,8},{8,12},{1,5},{5,9},{9,13},{2,6},{6,10},{10,14},{3,7},{... | collective-permute-start | bytes 368648 | tf_op jit(solution)/shard_map/ppermute | solution.py:14
  14.6 0.6 copy-done.3
  15.8 0.6 copy-done.4
  16.6 1.3 %slice_reduce_fusion.30 = (f32[16,16]{1,0:T(8,128)S(1)}, f32[16,16]{1,0:T(8,128)S(1)}, f32[16,16]{1,0:T(8,128)S(1)}, f32[16,16]{1,0:T(8,128)S(1)}, f32[16,16]{1,...) fusion(f32[1,16,16,1,31]{4,2,1,3,0:T(8,128)S(1)} %convolution_b, ...), kind=kLoop, calls=%fused_computation.756 | loop fusion | bytes 38912 | tf_op jit(solution)/shard_map/slice | solution.py:25
  18.4 0.9 %slice_reduce_fusion.29 = (f32[16,16]{1,0:T(8,128)S(1)}, f32[16,16]{1,0:T(8,128)S(1)}, f32[16,16]{1,0:T(8,128)S(1)}, f32[16,16]{1,0:T(8,128)S(1)}, f32[16,16]{1,...) fusion(f32[1,16,16,1,31]{4,2,1,3,0:T(8,128)S(1)} %convolution_b, ...), kind=kLoop, calls=%fused_computation.738 | loop fusion | bytes 24576 | tf_op jit(solution)/shard_map/slice | solution.py:25
  19.4 0.7 fusion.279
  20.1 2.3 %fusion.370 = f32[1,16,16,128]{3,2,1,0:T(8,128)S(1)} fusion(f32[1,16,16,128]{3,2,1,0:T(8,128)S(1)} %bitcast.93, f32[16,16,128]{2,1,0:T(8,128)S(1)} %fusion.279, f32[16,16]{1,0:T(8,128)S(1)} %get-tuple-element.6, f32[16,16]{1,0:T(8,128)S(1)} %get-tuple-element.7, f32[16,16]{1,0:T(8,128)S(1)} %get-tuple-element.8, f32[16,16]{1,0:T(8,128)S(1)} %get-tuple-element.9, ...), kind=kLoop, calls=%fused_computation.629 | loop fusion | flops 1998848 | bytes 424960 | tf_op jit(solution)/shard_map/add | solution.py:26
  22.4 1.5 %collective-permute-start.2 = (f32[1,15,16,128]{3,2,1,0:T(8,128)S(1)}, f32[1,15,16,128]{3,2,1,0:T(8,128)S(1)}, u32[]{:S(2)}, u32[]{:S(2)}) collective-permute-start(f32[1,15,16,128]{3,2,1,0:T(8,128)S(1)} %get-tuple-element.102), channel_id=1, source_target_pairs={{0,1},{1,2},{2,3},{4,5},{5,6},{6,7},{8,9},{9,10},{10,11},{12,13},{... | collective-permute-start | bytes 368648 | tf_op jit(solution)/shard_map/ppermute | solution.py:14
  23.9 1.4 %collective-permute-start.3 = (f32[1,15,16,128]{3,2,1,0:T(8,128)S(1)}, f32[1,15,16,128]{3,2,1,0:T(8,128)S(1)}, u32[]{:S(2)}, u32[]{:S(2)}) collective-permute-start(f32[1,15,16,128]{3,2,1,0:T(8,128)S(1)} %get-tuple-element.103), channel_id=1, source_target_pairs={{1,0},{2,1},{3,2},{5,4},{6,5},{7,6},{9,8},{10,9},{11,10},{13,12},{... | collective-permute-start | bytes 368648 | tf_op jit(solution)/shard_map/ppermute | solution.py:15
  25.4 3.8 %collective-permute-done.3 = f32[1,15,16,128]{3,2,1,0:T(8,128)S(1)} collective-permute-done((f32[1,15,16,128]{3,2,1,0:T(8,128)S(1)}, f32[1,15,16,128]{3,2,1,0:T(8,128)S(1)}, u32[]{:S(2)}, u32[]{:S(2)}) %collective-permute-start.3) | collective-permute-done | bytes 122912 | tf_op jit(solution)/shard_map/ppermute | solution.py:15
  29.3 0.3 fusion.90
  29.6 1.3 %collective-permute-start.4 = (f32[1,15,16,128]{3,2,1,0:T(8,128)S(1)}, f32[1,15,16,128]{3,2,1,0:T(8,128)S(1)}, u32[]{:S(2)}, u32[]{:S(2)}) collective-permute-start(f32[1,15,16,128]{3,2,1,0:T(8,128)S(1)} %get-tuple-element.100), channel_id=1, source_target_pairs={{1,0},{2,1},{3,2},{5,4},{6,5},{7,6},{9,8},{10,9},{11,10},{13,12},{... | collective-permute-start | bytes 368648 | tf_op jit(solution)/shard_map/ppermute | solution.py:15
  30.9 6.0 %collective-permute-start.5 = (f32[1,15,16,128]{3,2,1,0:T(8,128)S(1)}, f32[1,15,16,128]{3,2,1,0:T(8,128)S(1)}, u32[]{:S(2)}, u32[]{:S(2)}) collective-permute-start(f32[1,15,16,128]{3,2,1,0:T(8,128)S(1)} %get-tuple-element.101), channel_id=1, source_target_pairs={{0,1},{1,2},{2,3},{4,5},{5,6},{6,7},{8,9},{9,10},{10,11},{12,13},{... | collective-permute-start | bytes 368648 | tf_op jit(solution)/shard_map/ppermute | solution.py:14
  36.9 0.9 %collective-permute-done.5 = f32[1,15,16,128]{3,2,1,0:T(8,128)S(1)} collective-permute-done((f32[1,15,16,128]{3,2,1,0:T(8,128)S(1)}, f32[1,15,16,128]{3,2,1,0:T(8,128)S(1)}, u32[]{:S(2)}, u32[]{:S(2)}) %collective-permute-start.5) | collective-permute-done | bytes 122912 | tf_op jit(solution)/shard_map/ppermute | solution.py:14
  38.2 2.3 %fusion.430 = f32[1,16,16,128]{3,2,1,0:T(8,128)S(1)} fusion(f32[1,16,16,128]{3,2,1,0:T(8,128)S(1)} %fusion.3, f32[16,16]{1,0:T(8,128)S(1)} %get-tuple-element.21, f32[16,16]{1,0:T(8,128)S(1)} %get-tuple-element.6, f32[16,16]{1,0:T(8,128)S(1)} %get-tuple-element.7, f32[16,16]{1,0:T(8,128)S(1)} %get-tuple-element.8, f32[16,16]{1,0:T(8,128)S(1)} %get-tuple-element.9, ...), kind=kLoop, calls=%fused_computation.689 | loop fusion | flops 1998848 | bytes 293888 | tf_op jit(solution)/shard_map/add | solution.py:26
  40.5 1.3 %collective-permute-start.6 = (f32[1,16,15,128]{3,2,1,0:T(8,128)S(1)}, f32[1,16,15,128]{3,2,1,0:T(8,128)S(1)}, u32[]{:S(2)}, u32[]{:S(2)}) collective-permute-start(f32[1,16,15,128]{3,2,1,0:T(8,128)S(1)} %get-tuple-element.98), channel_id=1, source_target_pairs={{4,0},{8,4},{12,8},{5,1},{9,5},{13,9},{6,2},{10,6},{14,10},{7,3},{... | collective-permute-start | bytes 368648 | tf_op jit(solution)/shard_map/ppermute | solution.py:15
  41.8 4.6 %collective-permute-start.7 = (f32[1,16,15,128]{3,2,1,0:T(8,128)S(1)}, f32[1,16,15,128]{3,2,1,0:T(8,128)S(1)}, u32[]{:S(2)}, u32[]{:S(2)}) collective-permute-start(f32[1,16,15,128]{3,2,1,0:T(8,128)S(1)} %get-tuple-element.99), channel_id=1, source_target_pairs={{0,4},{4,8},{8,12},{1,5},{5,9},{9,13},{2,6},{6,10},{10,14},{3,7},{... | collective-permute-start | bytes 368648 | tf_op jit(solution)/shard_map/ppermute | solution.py:14
  46.4 1.0 %collective-permute-done.6 = f32[1,16,15,128]{3,2,1,0:T(8,128)S(1)} collective-permute-done((f32[1,16,15,128]{3,2,1,0:T(8,128)S(1)}, f32[1,16,15,128]{3,2,1,0:T(8,128)S(1)}, u32[]{:S(2)}, u32[]{:S(2)}) %collective-permute-start.6) | collective-permute-done | bytes 122912 | tf_op jit(solution)/shard_map/ppermute | solution.py:15
  47.4 1.5 %collective-permute-done.7 = f32[1,16,15,128]{3,2,1,0:T(8,128)S(1)} collective-permute-done((f32[1,16,15,128]{3,2,1,0:T(8,128)S(1)}, f32[1,16,15,128]{3,2,1,0:T(8,128)S(1)}, u32[]{:S(2)}, u32[]{:S(2)}) %collective-permute-start.7) | collective-permute-done | bytes 122912 | tf_op jit(solution)/shard_map/ppermute | solution.py:14
  48.9 1.4 %fusion.177 = f32[16,16,128]{2,1,0:T(8,128)} fusion(f32[1,16,15,128]{3,2,1,0:T(8,128)S(1)} %collective-permute-done.7, f32[1,16,16,128]{3,2,1,0:T(8,128)S(1)} %fusion.430, f32[1,16,15,128]{3,2,1,0:T(8,128)S(1)} %collective-permute-done.6, f32[16,128]{1,0:T(8,128)S(1)} %bitcast.97, f32[16,128]{1,0:T(8,128)S(1)} %bitcast.99, f32[16,128]{1,0:T(8,128)S(1)} %bitcast.101, ...), kind=kLoop, calls=%fused_computation.436 | loop fusion | flops 2981888 | bytes 761856 | tf_op jit(solution)/shard_map/reduce_sum | solution.py:62
  50.2 27.3 %all-reduce.4.cloned.1.call-done = f32[16,16,128]{2,1,0:T(8,128)} async-done(((f32[16,16,128]{2,1,0:T(8,128)}), f32[16,16,128]{2,1,0:T(8,128)}) %all-reduce.4.cloned.1.call-update) | async-done | bytes 131088 | tf_op jit(solution)/shard_map/psum | solution.py:63
  77.5 1.6 %multiply_multiply_fusion = f32[16,16,128]{2,1,0:T(8,128)} fusion(f32[16,16,128]{2,1,0:T(8,128)S(1)} %copy-done, f32[16,16,128]{2,1,0:T(8,128)} %all-reduce.4.cloned.1.call-done), kind=kLoop, calls=%fused_computation.757 | loop fusion | flops 65536 | bytes 393216 | tf_op jit(solution)/shard_map/div | solution.py:64
  (31 shorter events, 1.8 us)
Async XLA Ops:
  6.5 7.9 %copy-start.2 = (f32[1,3,16,31]{3,2,1,0:T(8,128)S(1)}, f32[1,3,16,31]{3,2,1,0:T(8,128)}, u32[]{:S(2)}) copy-start(f32[1,3,16,31]{3,2,1,0:T(8,128)} %param.11) | copy-start | bytes 17860
  6.5 71.0 %all-reduce.4.cloned.1.call-start = ((), (), s32[]{:S(2)}) async-start(), calls=%async_computation | async-start | bytes 262144 | tf_op jit(solution)/shard_map/psum | solution.py:63
  7.5 11.9 %collective-permute-start.1 = (f32[16,15,128]{2,1,0:T(8,128)S(1)}, f32[16,15,128]{2,1,0:T(8,128)S(1)}, u32[]{:S(2)}, u32[]{:S(2)}) collective-permute-start(f32[16,15,128]{2,1,0:T(8,128)S(1)} %get-tuple-element.104), channel_id=1, source_target_pairs={{4,0},{8,4},{12,8},{5,1},{9,5},{13,9},{6,2},{10,6},{14,10},{7,3},{... | collective-permute-start | bytes 368648 | tf_op jit(solution)/shard_map/ppermute | solution.py:15
  8.8 10.6 %collective-permute-start = (f32[16,15,128]{2,1,0:T(8,128)S(1)}, f32[16,15,128]{2,1,0:T(8,128)S(1)}, u32[]{:S(2)}, u32[]{:S(2)}) collective-permute-start(f32[16,15,128]{2,1,0:T(8,128)S(1)} %get-tuple-element.105), channel_id=1, source_target_pairs={{0,4},{4,8},{8,12},{1,5},{5,9},{9,13},{2,6},{6,10},{10,14},{3,7},{... | collective-permute-start | bytes 368648 | tf_op jit(solution)/shard_map/ppermute | solution.py:14
  14.5 0.7 copy-start.3
  15.7 0.7 copy-start.4
  16.6 1.4 %copy-start.5 = (s32[1,16,128]{2,1,0:T(8,128)S(1)}, s32[1,16,128]{2,1,0:T(8,128)}, u32[]{:S(2)}) copy-start(s32[1,16,128]{2,1,0:T(8,128)} %param.10) | copy-start | bytes 24580
  18.4 0.9 %copy-start = (f32[16,16,128]{2,1,0:T(8,128)S(1)}, f32[16,16,128]{2,1,0:T(8,128)}, u32[]{:S(2)}) copy-start(f32[16,16,128]{2,1,0:T(8,128)} %param.6) | copy-start | bytes 393220
  22.4 3.0 %collective-permute-start.2 = (f32[1,15,16,128]{3,2,1,0:T(8,128)S(1)}, f32[1,15,16,128]{3,2,1,0:T(8,128)S(1)}, u32[]{:S(2)}, u32[]{:S(2)}) collective-permute-start(f32[1,15,16,128]{3,2,1,0:T(8,128)S(1)} %get-tuple-element.102), channel_id=1, source_target_pairs={{0,1},{1,2},{2,3},{4,5},{5,6},{6,7},{8,9},{9,10},{10,11},{12,13},{... | collective-permute-start | bytes 368648 | tf_op jit(solution)/shard_map/ppermute | solution.py:14
  23.9 5.4 %copy-start.1 = (f32[1,16,16,128]{3,2,1,0:T(8,128)S(1)}, f32[1,16,16,128]{3,2,1,0:T(8,128)}, u32[]{:S(2)}) copy-start(f32[1,16,16,128]{3,2,1,0:T(8,128)} %param.7) | copy-start | bytes 393220
  23.9 5.4 %collective-permute-start.3 = (f32[1,15,16,128]{3,2,1,0:T(8,128)S(1)}, f32[1,15,16,128]{3,2,1,0:T(8,128)S(1)}, u32[]{:S(2)}, u32[]{:S(2)}) collective-permute-start(f32[1,15,16,128]{3,2,1,0:T(8,128)S(1)} %get-tuple-element.103), channel_id=1, source_target_pairs={{1,0},{2,1},{3,2},{5,4},{6,5},{7,6},{9,8},{10,9},{11,10},{13,12},{... | collective-permute-start | bytes 368648 | tf_op jit(solution)/shard_map/ppermute | solution.py:15
  29.6 7.3 %collective-permute-start.4 = (f32[1,15,16,128]{3,2,1,0:T(8,128)S(1)}, f32[1,15,16,128]{3,2,1,0:T(8,128)S(1)}, u32[]{:S(2)}, u32[]{:S(2)}) collective-permute-start(f32[1,15,16,128]{3,2,1,0:T(8,128)S(1)} %get-tuple-element.100), channel_id=1, source_target_pairs={{1,0},{2,1},{3,2},{5,4},{6,5},{7,6},{9,8},{10,9},{11,10},{13,12},{... | collective-permute-start | bytes 368648 | tf_op jit(solution)/shard_map/ppermute | solution.py:15
  30.9 7.0 %collective-permute-start.5 = (f32[1,15,16,128]{3,2,1,0:T(8,128)S(1)}, f32[1,15,16,128]{3,2,1,0:T(8,128)S(1)}, u32[]{:S(2)}, u32[]{:S(2)}) collective-permute-start(f32[1,15,16,128]{3,2,1,0:T(8,128)S(1)} %get-tuple-element.101), channel_id=1, source_target_pairs={{0,1},{1,2},{2,3},{4,5},{5,6},{6,7},{8,9},{9,10},{10,11},{12,13},{... | collective-permute-start | bytes 368648 | tf_op jit(solution)/shard_map/ppermute | solution.py:14
  40.5 6.9 %collective-permute-start.6 = (f32[1,16,15,128]{3,2,1,0:T(8,128)S(1)}, f32[1,16,15,128]{3,2,1,0:T(8,128)S(1)}, u32[]{:S(2)}, u32[]{:S(2)}) collective-permute-start(f32[1,16,15,128]{3,2,1,0:T(8,128)S(1)} %get-tuple-element.98), channel_id=1, source_target_pairs={{4,0},{8,4},{12,8},{5,1},{9,5},{13,9},{6,2},{10,6},{14,10},{7,3},{... | collective-permute-start | bytes 368648 | tf_op jit(solution)/shard_map/ppermute | solution.py:15
  41.8 7.1 %collective-permute-start.7 = (f32[1,16,15,128]{3,2,1,0:T(8,128)S(1)}, f32[1,16,15,128]{3,2,1,0:T(8,128)S(1)}, u32[]{:S(2)}, u32[]{:S(2)}) collective-permute-start(f32[1,16,15,128]{3,2,1,0:T(8,128)S(1)} %get-tuple-element.99), channel_id=1, source_target_pairs={{0,4},{4,8},{8,12},{1,5},{5,9},{9,13},{2,6},{6,10},{10,14},{3,7},{... | collective-permute-start | bytes 368648 | tf_op jit(solution)/shard_map/ppermute | solution.py:14
Sparse Core Ops, SparseCore 0:
  50.4 27.1 all-reduce.3
where the time goes:
time: 86.4 us; the launch traced here: 85.9 us
  waiting for transfers between devices  34.6 us (40%)
  starting transfers between devices  22.9 us (27%)
  between operations  13.7 us (16%)
  other arithmetic  8.97 us (10%)
  local copies, waits for them, and re-layouts  4.95 us (6%)
    psum x1, waiting for transfers between devices, shards(): total = lax.psum(local_sum, 'view')  27.3 us
    ppermute x4, starting transfers between devices, with_halo(): before = lax.ppermute(last, axis, up)  17.6 us
    add x4, other arithmetic, banded(): total = term if total is None else total + term  5.56 us
    ppermute x4, starting transfers between devices, with_halo(): after = lax.ppermute(initial, axis, down)  5.3 us
    ppermute x4, waiting for transfers between devices, with_halo(): after = lax.ppermute(initial, axis, down)  4.84 us
    slice x6, local copies, waits for them, and re-layouts, banded(): weights[..., k] * lax.slice_in_dim(padded, start, start + count, axis=dim)  2.63 us
    ppermute x4, waiting for transfers between devices, with_halo(): before = lax.ppermute(last, axis, up)  2.44 us
  transfers between devices with their start and end apart: 9, of which 5 were waited for; matrix products, arithmetic and copies ran while one was open for 4% of the time, Pallas kernels for 0%

commit v1 on v0

v1 whole, which is shorter than its diff:
```python
import functools

import jax
import jax.numpy as jnp
from jax import lax
from jax.experimental import pallas as pl
from jax.experimental.pallas import tpu as pltpu
from jax.sharding import PartitionSpec as P

MESH = pl.DeviceIdType.MESH
ROWS = 8
GROUP = 8


def total_of(terms):
    total = None
    for term in terms:
        total = term if total is None else total + term
    return total


class Halo:
    def __init__(self, buffer, axis, size, count, width, plane_pieces, row_pieces, rows, sems):
        self.buffer, self.axis, self.count, self.width = buffer, axis, count, width
        self.plane_pieces, self.row_pieces, self.rows = plane_pieces, row_pieces, rows
        self.send, self.recv = sems
        here = lax.axis_index(axis)
        self.has = (here > 0, here < size - 1)
        self.to = (lax.max(here - 1, 0), lax.min(here + 1, size - 1))

    def copy(self, way, piece, row_piece):
        length = self.count // self.plane_pieces
        low, high = piece * length, (piece + 1) * length
        if way == 0:
            high = min(high, self.width)
            landing = self.count + self.width + low
        else:
            low = max(low, self.count - self.width)
            landing = low - (self.count - self.width)
        depth = self.rows // self.row_pieces
        rows = pl.ds(row_piece * depth, depth)
        slot = (way * self.plane_pieces + piece) * self.row_pieces + row_piece
        return pltpu.make_async_remote_copy(
            src_ref=self.buffer.at[pl.ds(self.width + low, high - low), rows],
            dst_ref=self.buffer.at[pl.ds(landing, high - low), rows],
            send_sem=self.send.at[slot],
            recv_sem=self.recv.at[slot],
            device_id={self.axis: self.to[way]},
            device_id_type=MESH,
        )

    def start(self, piece, row_piece):
        for way in (0, 1):
            @pl.when(self.has[way])
            def _():
                self.copy(way, piece, row_piece).start()

    def arrive(self, piece, row_piece):
        for way in (0, 1):
            @pl.when(self.has[1 - way])
            def _():
                self.copy(way, piece, row_piece).wait_recv()

    def finish(self):
        for way in (0, 1):
            @pl.when(self.has[way])
            def _():
                for piece in range(self.plane_pieces):
                    for row_piece in range(self.row_pieces):
                        self.copy(way, piece, row_piece).wait_send()

    def clear_ends(self):
        blank = jnp.zeros((self.width,) + self.buffer.shape[1:], self.buffer.dtype)

        @pl.when(jnp.logical_not(self.has[0]))
        def _():
            self.buffer[: self.width] = blank

        @pl.when(jnp.logical_not(self.has[1]))
        def _():
            self.buffer[self.count + self.width : self.count + 2 * self.width] = blank


def kernel(
    sizes, est, rec, xi, yi, zi, prof, out,
    ebuf, zbuf, rbuf, gbuf, tbuf, vbuf, table_in, table, wx, wy, wz,
    e_send, e_recv, z_send, z_recv, r_send, r_recv, g_send, g_recv, v_send, v_recv,
):
    views, tiles, slabs = sizes
    nz, nx, ny = est.shape
    directions, profs, taps = prof.shape[1:]
    half = taps // 2
    zparts, xparts = nz // ROWS, nx // ROWS
    e_halo = Halo(ebuf, "tile", tiles, nx, half, 1, zparts, nz, (e_send, e_recv))
    z_halo = Halo(zbuf, "slab", slabs, nz, half, zparts, xparts, nx, (z_send, z_recv))
    r_halo = Halo(rbuf, "slab", slabs, nz, half, 1, xparts, nx, (r_send, r_recv))
    g_halo = Halo(gbuf, "tile", tiles, nx, half, xparts, zparts, nz, (g_send, g_recv))
    view = lax.axis_index("view")

    barrier = pltpu.get_barrier_semaphore()
    heard = views - 1
    for halo in (e_halo, z_halo):
        for way in (0, 1):
            heard = heard + halo.has[way].astype(jnp.int32)

            @pl.when(halo.has[way])
            def _():
                pl.semaphore_signal(barrier, inc=1, device_id={halo.axis: halo.to[way]}, device_id_type=MESH)
    for step in range(1, views):
        pl.semaphore_signal(
            barrier, inc=1, device_id={"view": lax.rem(view + step, views)}, device_id_type=MESH
        )

    flat_est = est.reshape(nz * nx, ny)
    for x in range(nx):
        for zp in range(zparts):
            ebuf[half + x, pl.ds(zp * ROWS, ROWS), :] = flat_est[pl.ds(zp * ROWS * nx + x, ROWS, stride=nx), :]
    for halo in (e_halo, z_halo, r_halo, g_halo):
        halo.clear_ends()
    table_in[...] = jnp.zeros(table_in.shape, table_in.dtype)
    for a in range(directions):
        profile = prof[0, a]
        table_in[pl.ds(a * profs, profs), pl.ds(0, taps)] = profile / jnp.sum(profile, axis=-1, keepdims=True)
    table[...] = table_in[...].T

    pl.semaphore_wait(barrier, heard)
    for zp in range(zparts):
        e_halo.start(0, zp)

    def tap(k, index):
        row = jnp.broadcast_to(table[pl.ds(k, 1), :], (ROWS, table.shape[1]))
        return jnp.take_along_axis(row, index, axis=1, mode="promise_in_bounds")

    for zp in range(zparts):
        rows = pl.ds(zp * ROWS, ROWS)
        index = xi[0, rows, :]
        for k in range(taps):
            wx[k, rows, :] = tap(k, index)
    lane = lax.broadcasted_iota(jnp.int32, (ROWS, ny), 1)
    for zp in range(zparts):
        rows = pl.ds(zp * ROWS, ROWS)
        lines = yi[0, rows, :]
        for x in range(nx):
            index = jnp.broadcast_to(lines[:, x : x + 1], (ROWS, ny)) + profs
            for k in range(taps):
                read = lane + (k - half)
                wy[k, x, rows, :] = jnp.where((read >= 0) & (read < ny), tap(k, index), 0.0)
    for xp in range(xparts):
        rows = pl.ds(xp * ROWS, ROWS)
        index = zi[0, rows, :] + 2 * profs
        for k in range(taps):
            wz[k, rows, :] = tap(k, index)

    def blur(field, weights, first, rows, adjoint):
        taps_here = [weights[k, rows, :] for k in range(taps)]
        reads = [field[first + i, rows, :] for i in range(GROUP + taps - 1)]
        return [
            total_of(taps_here[k] * reads[i + (taps - 1 - k if adjoint else k)] for k in range(taps))
            for i in range(GROUP)
        ]

    flat_z = zbuf.reshape(zbuf.shape[0] * nx, ny)
    for zp in range(zparts):
        e_halo.arrive(0, zp)
        rows = pl.ds(zp * ROWS, ROWS)

        def forward(g, carry):
            first = g * GROUP
            for i, line in enumerate(blur(ebuf, wx, first, rows, False)):
                along_y = total_of(
                    wy[k, first + i, rows, :] * pltpu.roll(line, (half - k) % ny, 1) for k in range(taps)
                )
                flat_z[pl.ds((half + zp * ROWS) * nx + first + i, ROWS, stride=nx), :] = along_y
            return carry

        lax.fori_loop(0, nx // GROUP, forward, 0)
        for xp in range(xparts):
            z_halo.start(zp, xp)

    for xp in range(xparts):
        for zp in range(zparts):
            z_halo.arrive(zp, xp)
        rows = pl.ds(xp * ROWS, ROWS)

        def divide(g, carry):
            first = g * GROUP
            for i, blurred in enumerate(blur(zbuf, wz, first, rows, False)):
                rbuf[half + first + i, rows, :] = rec[0, first + i, rows, :] / blurred
            return carry

        lax.fori_loop(0, nz // GROUP, divide, 0)
        r_halo.start(0, xp)

    flat_t = tbuf.reshape(nz * nx, ny)
    for xp in range(xparts):
        r_halo.arrive(0, xp)
        rows = pl.ds(xp * ROWS, ROWS)

        def back_z(g, carry):
            first = g * GROUP
            for i, line in enumerate(blur(rbuf, wz, first, rows, True)):
                tbuf[first + i, rows, :] = line
            return carry

        lax.fori_loop(0, nz // GROUP, back_z, 0)
        for zp in range(zparts):
            z_rows = pl.ds(zp * ROWS, ROWS)

            def back_y(i, carry):
                x = xp * ROWS + i
                line = flat_t[pl.ds(zp * ROWS * nx + x, ROWS, stride=nx), :]
                gbuf[half + x, z_rows, :] = total_of(
                    pltpu.roll(wy[k, x, z_rows, :] * line, (k - half) % ny, 1) for k in range(taps)
                )
                return carry

            lax.fori_loop(0, ROWS, back_y, 0, unroll=4)
            g_halo.start(xp, zp)

    def view_copy(step, zp):
        piece = vbuf.at[view, pl.ds(zp * ROWS, ROWS)]
        slot = (step - 1) * zparts + zp
        return pltpu.make_async_remote_copy(
            src_ref=piece, dst_ref=piece, send_sem=v_send.at[slot], recv_sem=v_recv.at[slot],
            device_id={"view": lax.rem(view + step, views)}, device_id_type=MESH,
        )

    flat_v = vbuf.reshape(views * nz * nx, ny)
    for zp in range(zparts):
        for xp in range(xparts):
            g_halo.arrive(xp, zp)
        rows = pl.ds(zp * ROWS, ROWS)

        def back_x(g, carry):
            first = g * GROUP
            for i, line in enumerate(blur(gbuf, wx, first, rows, True)):
                flat_v[pl.ds((view * nz + zp * ROWS) * nx + first + i, ROWS, stride=nx), :] = line
            return carry

        lax.fori_loop(0, nx // GROUP, back_x, 0)
        for step in range(1, views):
            view_copy(step, zp).start()

    for zp in range(zparts):
        for step in range(1, views):
            view_copy(step, zp).wait_recv()
        planes = pl.ds(zp * ROWS, ROWS)
        out[planes] = est[planes] * total_of(vbuf[v, planes] for v in range(views)) / views

    for halo in (e_halo, z_halo, r_halo, g_halo):
        halo.finish()
    for zp in range(zparts):
        for step in range(1, views):
            view_copy(step, zp).wait_send()


def shards(sizes, estimate, recorded, x_index, y_index, z_index, profiles):
    views = sizes[0]
    nz, nx, ny = estimate.shape
    directions, profs, taps = profiles.shape[1:]
    assert recorded.shape[0] == 1
    half = taps // 2
    assert half <= min(nz, nx)
    assert directions * profs <= 128
    zparts, xparts = nz // ROWS, nx // ROWS
    f32 = jnp.float32
    counts = (zparts, zparts * xparts, xparts, zparts * xparts)
    sems = [pltpu.SemaphoreType.DMA((2 * c,)) for c in counts for _ in range(2)]
    sems += [pltpu.SemaphoreType.DMA((max(1, views - 1) * zparts,)) for _ in range(2)]
    return pl.pallas_call(
        functools.partial(kernel, sizes),
        out_shape=jax.ShapeDtypeStruct(estimate.shape, f32),
        in_specs=[pl.BlockSpec(memory_space=pltpu.VMEM)] * 6,
        out_specs=pl.BlockSpec(memory_space=pltpu.VMEM),
        scratch_shapes=[
            pltpu.VMEM((nx + 2 * half, nz, ny), f32),
            pltpu.VMEM((nz + 2 * half, nx, ny), f32),
            pltpu.VMEM((nz + 2 * half, nx, ny), f32),
            pltpu.VMEM((nx + 2 * half, nz, ny), f32),
            pltpu.VMEM((nz, nx, ny), f32),
            pltpu.VMEM((views, nz, nx, ny), f32),
            pltpu.VMEM((128, 128), f32),
            pltpu.VMEM((128, 128), f32),
            pltpu.VMEM((taps, nz, ny), f32),
            pltpu.VMEM((taps, nx, nz, ny), f32),
            pltpu.VMEM((taps, nx, ny), f32),
            *sems,
        ],
        compiler_params=pltpu.CompilerParams(
            collective_id=0, has_side_effects=True, vmem_limit_bytes=32 * 1024 * 1024
        ),
    )(estimate, recorded, x_index, y_index, z_index, profiles)


def solution(mesh):
    sizes = tuple(mesh.shape[name] for name in ("view", "tile", "slab"))
    placed = (
        P("slab", "tile", None),
        P("view", "slab", "tile", None),
        P("view", "slab", None),
        P("view", "slab", "tile"),
        P("view", "tile", None),
        P("view", None, None, None),
    )
    return jax.shard_map(
        functools.partial(shards, sizes),
        mesh=mesh, in_specs=placed, out_specs=P("slab", "tile", None), check_vma=False,
    )
```

time: 86.4 us -> 30.1 us (0.35)
  waiting for transfers between devices: 34.6 us -> 0 us
  Pallas kernels: 0 us -> 24.5 us
  starting transfers between devices: 22.9 us -> 0 us
  between operations: 13.7 us -> 0.02 us
  other arithmetic: 8.97 us -> 0 us
    psum x1 -> x0, waiting for transfers between devices: 27.3 us -> none  [shards(): total = lax.psum(local_sum, 'view')]
    pallas_call x0 -> x1, Pallas kernels: none -> 24.5 us  [shards(): pl.pallas_call(functools.partial(kernel, sizes), out_shape=jax.ShapeDtype...]
    ppermute x8 -> x0, starting transfers between devices: 22.9 us -> none  [the longest x4 17.6 us: with_halo(): before = lax.ppermute(last, axis, up)]
    ppermute x8 -> x0, waiting for transfers between devices: 7.28 us -> none  [the longest x4 4.84 us: with_halo(): after = lax.ppermute(initial, axis, down)]
    add x4 -> x0, other arithmetic: 5.56 us -> none  [banded(): total = term if total is None else total + term]
    unnamed x13, local copies, waits for them, and re-layouts: 1.26 us -> 5.29 us
    slice x10 -> x0, local copies, waits for them, and re-layouts: 3.68 us -> none  [the longest x6 2.63 us: banded(): weights[..., k] * lax.slice_in_dim(padded, start, start + count, axis=dim)]
    div x3 -> x0, other arithmetic: 1.98 us -> none  [the longest x1 1.58 us: shards(): return estimate * total / (views_here * lax.axis_size('view'))]
  transfers between devices with their start and end apart: 9 -> 0, of which waited for: 5 -> 0; matrix products, arithmetic and copies ran while one was open for 4% -> 0% of each run, Pallas kernels for 0% -> 0%
where the time goes in v1:
time: 30.1 us; the launch traced here: 29.8 us
  Pallas kernels  24.5 us (81%)
  local copies, waits for them, and re-layouts  5.29 us (18%)
    pallas_call x1, Pallas kernels, shards(): pl.pallas_call(functools.partial(kernel, sizes), out_shape=jax.ShapeDtype...  24.5 us
    unnamed x13, local copies, waits for them, and re-layouts  5.29 us

profile of v1, /device:TPU:0, one launch (start us, length us, event | category | flops | bytes accessed | tf_op | source)
XLA Modules:
  0.0 29.8 jit_solution(17449641101826615322)
XLA Ops:
  0.0 0.0 copy-start
  0.0 0.9 %copy-done = f32[16,16,128]{2,1,0:T(8,128)S(1)} copy-done((f32[16,16,128]{2,1,0:T(8,128)S(1)}, f32[16,16,128]{2,1,0:T(8,128)}, u32[]{:S(2)}) %copy-start) | copy-done | bytes 131096
  0.9 0.0 copy-start.1
  0.9 0.9 %copy-done.1 = f32[1,16,16,128]{3,2,1,0:T(8,128)S(1)} copy-done((f32[1,16,16,128]{3,2,1,0:T(8,128)S(1)}, f32[1,16,16,128]{3,2,1,0:T(8,128)}, u32[]{:S(2)}) %copy-start.1) | copy-done | bytes 131096
  1.8 0.0 copy-start.2
  1.8 0.7 %copy-done.2 = f32[1,3,16,31]{3,2,1,0:T(8,128)S(1)} copy-done((f32[1,3,16,31]{3,2,1,0:T(8,128)S(1)}, f32[1,3,16,31]{3,2,1,0:T(8,128)}, u32[]{:S(2)}) %copy-start.2) | copy-done | bytes 5976
  2.5 0.0 copy-start.3
  2.5 0.7 %copy-done.3 = s32[1,16,128]{2,1,0:T(8,128)S(1)} copy-done((s32[1,16,128]{2,1,0:T(8,128)S(1)}, s32[1,16,128]{2,1,0:T(8,128)}, u32[]{:S(2)}) %copy-start.3) | copy-done | bytes 8216
  3.2 0.0 copy-start.4
  3.2 0.7 %copy-done.4 = s32[1,16,16]{2,1,0:T(8,128)S(1)} copy-done((s32[1,16,16]{2,1,0:T(8,128)S(1)}, s32[1,16,16]{2,1,0:T(8,128)}, u32[]{:S(2)}) %copy-start.4) | copy-done | bytes 1048
  3.9 0.0 copy-start.5
  3.9 0.7 %copy-done.5 = s32[1,16,128]{2,1,0:T(8,128)S(1)} copy-done((s32[1,16,128]{2,1,0:T(8,128)S(1)}, s32[1,16,128]{2,1,0:T(8,128)}, u32[]{:S(2)}) %copy-start.5) | copy-done | bytes 8216
  4.6 24.5 %shard_map.64 = f32[16,16,128]{2,1,0:T(8,128)S(1)} custom-call(f32[16,16,128]{2,1,0:T(8,128)S(1)} %copy-done, f32[1,16,16,128]{3,2,1,0:T(8,128)S(1)} %copy-done.1, s32[1,16,128]{2,1,0:T(8,128)S(1)} %copy-done.3, s32[1,16,16]{2,1,0:T(8,128)S(1)} %copy-done.4, s32[1,16,128]{2,1,0:T(8,128)S(1)} %copy-done.5, f32[1,3,16,31]{3,2,1,0:T(8,128)S(1)} %copy-done.2), custom_call_target="tpu_custom_call" | custom-call | tf_op jit(solution)/shard_map/pallas_call | solution.py:270
  29.1 0.7 %copy.8 = f32[16,16,128]{2,1,0:T(8,128)} copy(f32[16,16,128]{2,1,0:T(8,128)S(1)} %shard_map.64) | data formatting | bytes 262144
Async XLA Ops:
  0.0 0.9 %copy-start = (f32[16,16,128]{2,1,0:T(8,128)S(1)}, f32[16,16,128]{2,1,0:T(8,128)}, u32[]{:S(2)}) copy-start(f32[16,16,128]{2,1,0:T(8,128)} %est.1) | copy-start | bytes 393220
  0.9 0.9 %copy-start.1 = (f32[1,16,16,128]{3,2,1,0:T(8,128)S(1)}, f32[1,16,16,128]{3,2,1,0:T(8,128)}, u32[]{:S(2)}) copy-start(f32[1,16,16,128]{3,2,1,0:T(8,128)} %rec.1) | copy-start | bytes 393220
  1.8 0.7 %copy-start.2 = (f32[1,3,16,31]{3,2,1,0:T(8,128)S(1)}, f32[1,3,16,31]{3,2,1,0:T(8,128)}, u32[]{:S(2)}) copy-start(f32[1,3,16,31]{3,2,1,0:T(8,128)} %prof.1) | copy-start | bytes 17860
  2.5 0.7 %copy-start.3 = (s32[1,16,128]{2,1,0:T(8,128)S(1)}, s32[1,16,128]{2,1,0:T(8,128)}, u32[]{:S(2)}) copy-start(s32[1,16,128]{2,1,0:T(8,128)} %xi.1) | copy-start | bytes 24580
  3.2 0.7 %copy-start.4 = (s32[1,16,16]{2,1,0:T(8,128)S(1)}, s32[1,16,16]{2,1,0:T(8,128)}, u32[]{:S(2)}) copy-start(s32[1,16,16]{2,1,0:T(8,128)} %yi.1) | copy-start | bytes 3076
  3.9 0.7 %copy-start.5 = (s32[1,16,128]{2,1,0:T(8,128)S(1)}, s32[1,16,128]{2,1,0:T(8,128)}, u32[]{:S(2)}) copy-start(s32[1,16,128]{2,1,0:T(8,128)} %zi.1) | copy-start | bytes 24580

commit v2 on v1

--- a/solution.py
+++ b/solution.py
@@ -82,11 +82,19 @@
 
 
 def kernel(
-    sizes, est, rec, xi, yi, zi, prof, out,
-    ebuf, zbuf, rbuf, gbuf, tbuf, vbuf, table_in, table, wx, wy, wz,
+    sizes, est_hbm, rec_hbm, xi_hbm, yi_hbm, zi_hbm, prof_hbm, out,
+    est, rec, xi, yi, zi, prof, in_sems, ebuf, zbuf, rbuf, gbuf, tbuf, vbuf, table_in, table, wx, wy, wz,
     e_send, e_recv, z_send, z_recv, r_send, r_recv, g_send, g_recv, v_send, v_recv,
 ):
     views, tiles, slabs = sizes
+    sources = (est_hbm, prof_hbm, xi_hbm, yi_hbm, zi_hbm, rec_hbm)
+    fetches = [
+        pltpu.make_async_copy(source, target, in_sems.at[i])
+        for i, (source, target) in enumerate(zip(sources, (est, prof, xi, yi, zi, rec)))
+    ]
+    for fetch in fetches:
+        fetch.start()
+    fetch_est, *fetch_taps, fetch_rec = fetches
     nz, nx, ny = est.shape
     directions, profs, taps = prof.shape[1:]
     half = taps // 2
@@ -111,12 +119,15 @@
             barrier, inc=1, device_id={"view": lax.rem(view + step, views)}, device_id_type=MESH
         )
 
+    fetch_est.wait()
     flat_est = est.reshape(nz * nx, ny)
     for x in range(nx):
         for zp in range(zparts):
             ebuf[half + x, pl.ds(zp * ROWS, ROWS), :] = flat_est[pl.ds(zp * ROWS * nx + x, ROWS, stride=nx), :]
     for halo in (e_halo, z_halo, r_halo, g_halo):
         halo.clear_ends()
+    for fetch in fetch_taps:
+        fetch.wait()
     table_in[...] = jnp.zeros(table_in.shape, table_in.dtype)
     for a in range(directions):
         profile = prof[0, a]
@@ -159,6 +170,7 @@
             for i in range(GROUP)
         ]
 
+    fetch_rec.wait()
     flat_z = zbuf.reshape(zbuf.shape[0] * nx, ny)
     for zp in range(zparts):
         e_halo.arrive(0, zp)
@@ -254,7 +266,8 @@
             view_copy(step, zp).wait_send()
 
 
-def shards(sizes, estimate, recorded, x_index, y_index, z_index, profiles):
+def shards(sizes, *args):
+    estimate, recorded, x_index, y_index, z_index, profiles = args
     views = sizes[0]
     nz, nx, ny = estimate.shape
     directions, profs, taps = profiles.shape[1:]
@@ -270,9 +283,11 @@
     return pl.pallas_call(
         functools.partial(kernel, sizes),
         out_shape=jax.ShapeDtypeStruct(estimate.shape, f32),
-        in_specs=[pl.BlockSpec(memory_space=pltpu.VMEM)] * 6,
+        in_specs=[pl.BlockSpec(memory_space=pltpu.HBM)] * 6,
         out_specs=pl.BlockSpec(memory_space=pltpu.VMEM),
         scratch_shapes=[
+            *(pltpu.VMEM(a.shape, a.dtype) for a in args),
+            pltpu.SemaphoreType.DMA((len(args),)),
             pltpu.VMEM((nx + 2 * half, nz, ny), f32),
             pltpu.VMEM((nz + 2 * half, nx, ny), f32),
             pltpu.VMEM((nz + 2 * half, nx, ny), f32),
@@ -287,9 +302,9 @@
             *sems,
         ],
         compiler_params=pltpu.CompilerParams(
-            collective_id=0, has_side_effects=True, vmem_limit_bytes=32 * 1024 * 1024
+            collective_id=0, has_side_effects=True, vmem_limit_bytes=67_043_328
         ),
-    )(estimate, recorded, x_index, y_index, z_index, profiles)
+    )(*args)
 
 
 def solution(mesh):

time: 30.1 us -> 26.9 us (0.89)
  local copies, waits for them, and re-layouts: 5.29 us -> 1.57 us
  Pallas kernels: 24.5 us -> 25.2 us
    unnamed x13 -> x1, local copies, waits for them, and re-layouts: 5.29 us -> 1.57 us
    pallas_call x1, Pallas kernels: 24.5 us -> 25.2 us  [shards(): pl.pallas_call(functools.partial(kernel, sizes), out_shape=jax.ShapeDtype...]
where the time goes in v2:
time: 26.9 us; the launch traced here: 26.7 us
  Pallas kernels  25.2 us (94%)
  local copies, waits for them, and re-layouts  1.57 us (6%)
    pallas_call x1, Pallas kernels, shards(): pl.pallas_call(functools.partial(kernel, sizes), out_shape=jax.ShapeDtype...  25.2 us
    unnamed x1, local copies, waits for them, and re-layouts  1.57 us

profile of v2, /device:TPU:0, one launch (start us, length us, event | category | flops | bytes accessed | tf_op | source)
XLA Modules:
  0.0 26.7 jit_solution(7746543252330478230)
XLA Ops:
  0.0 25.2 %shard_map.64 = f32[16,16,128]{2,1,0:T(8,128)} custom-call(f32[16,16,128]{2,1,0:T(8,128)} %est_hbm.1, f32[1,16,16,128]{3,2,1,0:T(8,128)} %rec_hbm.1, s32[1,16,128]{2,1,0:T(8,128)} %xi_hbm.1, s32[1,16,16]{2,1,0:T(8,128)} %yi_hbm.1, s32[1,16,128]{2,1,0:T(8,128)} %zi_hbm.1, f32[1,3,16,31]{3,2,1,0:T(8,128)} %prof_hbm.1), custom_call_target="tpu_custom_call" | custom-call | tf_op jit(solution)/shard_map/pallas_call | solution.py:283
  25.2 1.6 %copy.8 = f32[16,16,128]{2,1,0:T(8,128)} copy(f32[16,16,128]{2,1,0:T(8,128)} %shard_map.64) | data formatting | bytes 262144

commit v3 on v2

--- a/solution.py
+++ b/solution.py
@@ -17,6 +17,16 @@
     for term in terms:
         total = term if total is None else total + term
     return total
+
+
+def estimate_copy(halo, source, landing, sems, way, piece):
+    planes = pl.ds(piece * ROWS, ROWS)
+    slot = way * (source.shape[0] // ROWS) + piece
+    return pltpu.make_async_remote_copy(
+        src_ref=source.at[planes], dst_ref=landing.at[way, planes],
+        send_sem=sems[0].at[slot], recv_sem=sems[1].at[slot],
+        device_id={halo.axis: halo.to[way]}, device_id_type=MESH,
+    )
 
 
 class Halo:
@@ -83,7 +93,7 @@
 
 def kernel(
     sizes, est_hbm, rec_hbm, xi_hbm, yi_hbm, zi_hbm, prof_hbm, out,
-    est, rec, xi, yi, zi, prof, in_sems, ebuf, zbuf, rbuf, gbuf, tbuf, vbuf, table_in, table, wx, wy, wz,
+    est, rec, xi, yi, zi, prof, in_sems, eland, ebuf, zbuf, rbuf, gbuf, tbuf, vbuf, table_in, table, wx, wy, wz,
     e_send, e_recv, z_send, z_recv, r_send, r_recv, g_send, g_recv, v_send, v_recv,
 ):
     views, tiles, slabs = sizes
@@ -99,7 +109,6 @@
     directions, profs, taps = prof.shape[1:]
     half = taps // 2
     zparts, xparts = nz // ROWS, nx // ROWS
-    e_halo = Halo(ebuf, "tile", tiles, nx, half, 1, zparts, nz, (e_send, e_recv))
     z_halo = Halo(zbuf, "slab", slabs, nz, half, zparts, xparts, nx, (z_send, z_recv))
     r_halo = Halo(rbuf, "slab", slabs, nz, half, 1, xparts, nx, (r_send, r_recv))
     g_halo = Halo(gbuf, "tile", tiles, nx, half, xparts, zparts, nz, (g_send, g_recv))
@@ -107,7 +116,7 @@
 
     barrier = pltpu.get_barrier_semaphore()
     heard = views - 1
-    for halo in (e_halo, z_halo):
+    for halo in (g_halo, z_halo):
         for way in (0, 1):
             heard = heard + halo.has[way].astype(jnp.int32)
 
@@ -119,12 +128,15 @@
             barrier, inc=1, device_id={"view": lax.rem(view + step, views)}, device_id_type=MESH
         )
 
-    fetch_est.wait()
-    flat_est = est.reshape(nz * nx, ny)
-    for x in range(nx):
-        for zp in range(zparts):
-            ebuf[half + x, pl.ds(zp * ROWS, ROWS), :] = flat_est[pl.ds(zp * ROWS * nx + x, ROWS, stride=nx), :]
-    for halo in (e_halo, z_halo, r_halo, g_halo):
+    pl.semaphore_wait(barrier, heard)
+    e_copy = functools.partial(estimate_copy, g_halo, est_hbm, eland, (e_send, e_recv))
+    for zp in range(zparts):
+        for way in (0, 1):
+            @pl.when(g_halo.has[way])
+            def _():
+                e_copy(way, zp).start()
+
+    for halo in (z_halo, r_halo, g_halo):
         halo.clear_ends()
     for fetch in fetch_taps:
         fetch.wait()
@@ -134,9 +146,32 @@
         table_in[pl.ds(a * profs, profs), pl.ds(0, taps)] = profile / jnp.sum(profile, axis=-1, keepdims=True)
     table[...] = table_in[...].T
 
-    pl.semaphore_wait(barrier, heard)
-    for zp in range(zparts):
-        e_halo.start(0, zp)
+    steps = int(taps**0.5) + 1
+
+    def coarse_of(k):
+        return (k - half) // steps * steps
+
+    def y_forward(line, x, rows):
+        shifted, partial = {}, {}
+        for k in range(taps):
+            coarse = coarse_of(k)
+            fine = k - half - coarse
+            if fine not in shifted:
+                shifted[fine] = pltpu.roll(line, -fine % ny, 1) if fine else line
+            term = wy[k, x, rows, :] * shifted[fine]
+            partial[coarse] = partial[coarse] + term if coarse in partial else term
+        return total_of(pltpu.roll(v, -c % ny, 1) if c else v for c, v in partial.items())
+
+    def y_back(line, x, rows):
+        shifted, partial = {}, {}
+        for k in range(taps):
+            coarse = coarse_of(k)
+            fine = k - half - coarse
+            if coarse not in shifted:
+                shifted[coarse] = pltpu.roll(line, coarse % ny, 1) if coarse else line
+            term = wy[k, x, rows, :] * shifted[coarse]
+            partial[fine] = partial[fine] + term if fine in partial else term
+        return total_of(pltpu.roll(v, f, 1) if f else v for f, v in partial.items())
 
     def tap(k, index):
         row = jnp.broadcast_to(table[pl.ds(k, 1), :], (ROWS, table.shape[1]))
@@ -148,14 +183,17 @@
         for k in range(taps):
             wx[k, rows, :] = tap(k, index)
     lane = lax.broadcasted_iota(jnp.int32, (ROWS, ny), 1)
+    inside = []
+    for k in range(taps):
+        read = lax.rem(lane + (ny - coarse_of(k)), ny) + (k - half)
+        inside.append((read >= 0) & (read < ny))
     for zp in range(zparts):
         rows = pl.ds(zp * ROWS, ROWS)
         lines = yi[0, rows, :]
         for x in range(nx):
             index = jnp.broadcast_to(lines[:, x : x + 1], (ROWS, ny)) + profs
             for k in range(taps):
-                read = lane + (k - half)
-                wy[k, x, rows, :] = jnp.where((read >= 0) & (read < ny), tap(k, index), 0.0)
+                wy[k, x, rows, :] = jnp.where(inside[k], tap(k, index), 0.0)
     for xp in range(xparts):
         rows = pl.ds(xp * ROWS, ROWS)
         index = zi[0, rows, :] + 2 * profs
@@ -170,19 +208,33 @@
             for i in range(GROUP)
         ]
 
+    def turn(source, planes, zp, first, at):
+        for i in range(planes):
+            line = source[pl.ds(zp * ROWS * nx + first + i, ROWS, stride=nx), :]
+            ebuf[at + i, pl.ds(zp * ROWS, ROWS), :] = line
+
+    fetch_est.wait()
+    for zp in range(zparts):
+        turn(est.reshape(nz * nx, ny), nx, zp, 0, half)
     fetch_rec.wait()
     flat_z = zbuf.reshape(zbuf.shape[0] * nx, ny)
     for zp in range(zparts):
-        e_halo.arrive(0, zp)
         rows = pl.ds(zp * ROWS, ROWS)
+        for way, first, at in ((0, 0, half + nx), (1, nx - half, 0)):
+            @pl.when(g_halo.has[1 - way])
+            def _():
+                e_copy(way, zp).wait_recv()
+                turn(eland.at[way].reshape(nz * nx, ny), half, zp, first, at)
+
+            @pl.when(jnp.logical_not(g_halo.has[1 - way]))
+            def _():
+                ebuf[at : at + half, rows, :] = jnp.zeros((half, ROWS, ny), ebuf.dtype)
 
         def forward(g, carry):
             first = g * GROUP
             for i, line in enumerate(blur(ebuf, wx, first, rows, False)):
-                along_y = total_of(
-                    wy[k, first + i, rows, :] * pltpu.roll(line, (half - k) % ny, 1) for k in range(taps)
-                )
-                flat_z[pl.ds((half + zp * ROWS) * nx + first + i, ROWS, stride=nx), :] = along_y
+                spot = (half + zp * ROWS) * nx + first + i
+                flat_z[pl.ds(spot, ROWS, stride=nx), :] = y_forward(line, first + i, rows)
             return carry
 
         lax.fori_loop(0, nx // GROUP, forward, 0)
@@ -204,26 +256,25 @@
         r_halo.start(0, xp)
 
     flat_t = tbuf.reshape(nz * nx, ny)
-    for xp in range(xparts):
-        r_halo.arrive(0, xp)
-        rows = pl.ds(xp * ROWS, ROWS)
-
-        def back_z(g, carry):
-            first = g * GROUP
-            for i, line in enumerate(blur(rbuf, wz, first, rows, True)):
-                tbuf[first + i, rows, :] = line
-            return carry
-
-        lax.fori_loop(0, nz // GROUP, back_z, 0)
-        for zp in range(zparts):
-            z_rows = pl.ds(zp * ROWS, ROWS)
+    for zp in range(zparts):
+        z_rows = pl.ds(zp * ROWS, ROWS)
+        for xp in range(xparts):
+            rows = pl.ds(xp * ROWS, ROWS)
+
+            def back_z(g, carry):
+                first = g * GROUP
+                for i, line in enumerate(blur(rbuf, wz, first, rows, True)):
+                    tbuf[first + i, rows, :] = line
+                return carry
+
+            if zp == 0:
+                r_halo.arrive(0, xp)
+                lax.fori_loop(0, nz // GROUP, back_z, 0)
 
             def back_y(i, carry):
                 x = xp * ROWS + i
                 line = flat_t[pl.ds(zp * ROWS * nx + x, ROWS, stride=nx), :]
-                gbuf[half + x, z_rows, :] = total_of(
-                    pltpu.roll(wy[k, x, z_rows, :] * line, (k - half) % ny, 1) for k in range(taps)
-                )
+                gbuf[half + x, z_rows, :] = y_back(line, x, z_rows)
                 return carry
 
             lax.fori_loop(0, ROWS, back_y, 0, unroll=4)
@@ -259,8 +310,13 @@
         planes = pl.ds(zp * ROWS, ROWS)
         out[planes] = est[planes] * total_of(vbuf[v, planes] for v in range(views)) / views
 
-    for halo in (e_halo, z_halo, r_halo, g_halo):
+    for halo in (z_halo, r_halo, g_halo):
         halo.finish()
+    for way in (0, 1):
+        @pl.when(g_halo.has[way])
+        def _():
+            for zp in range(zparts):
+                e_copy(way, zp).wait_send()
     for zp in range(zparts):
         for step in range(1, views):
             view_copy(step, zp).wait_send()
@@ -288,6 +344,7 @@
         scratch_shapes=[
             *(pltpu.VMEM(a.shape, a.dtype) for a in args),
             pltpu.SemaphoreType.DMA((len(args),)),
+            pltpu.VMEM((2, nz, nx, ny), f32),
             pltpu.VMEM((nx + 2 * half, nz, ny), f32),
             pltpu.VMEM((nz + 2 * half, nx, ny), f32),
             pltpu.VMEM((nz + 2 * half, nx, ny), f32),
@@ -302,9 +359,9 @@
             *sems,
         ],
         compiler_params=pltpu.CompilerParams(
-            collective_id=0, has_side_effects=True, vmem_limit_bytes=67_043_328
+            collective_id=0, has_side_effects=True, vmem_limit_bytes=32 * 1024 * 1024
         ),
-    )(*args)
+    )(*(pltpu.with_memory_space_constraint(a, pltpu.HBM) for a in args))
 
 
 def solution(mesh):

time: 26.9 us -> 24.9 us (0.926)
  Pallas kernels: 25.2 us -> 24.1 us
  local copies, waits for them, and re-layouts: 1.57 us -> 0.66 us
    pallas_call x1, Pallas kernels: 25.2 us -> 24.1 us  [shards(): pl.pallas_call(functools.partial(kernel, sizes), out_shape=jax.ShapeDtype...]
    unnamed x1, local copies, waits for them, and re-layouts: 1.57 us -> 0.66 us
where the time goes in v3:
time: 24.9 us; the launch traced here: 24.8 us
  Pallas kernels  24.1 us (97%)
  local copies, waits for them, and re-layouts  0.66 us (3%)
    pallas_call x1, Pallas kernels, shards(): pl.pallas_call(functools.partial(kernel, sizes), out_shape=jax.ShapeDtype...  24.1 us
    unnamed x1, local copies, waits for them, and re-layouts  0.66 us

profile of v3, /device:TPU:0, one launch (start us, length us, event | category | flops | bytes accessed | tf_op | source)
XLA Modules:
  0.0 24.8 jit_solution(2394449192837259792)
XLA Ops:
  0.0 24.1 %shard_map.64 = f32[16,16,128]{2,1,0:T(8,128)S(1)} custom-call(f32[16,16,128]{2,1,0:T(8,128)} %est_hbm.1, f32[1,16,16,128]{3,2,1,0:T(8,128)} %rec_hbm.1, s32[1,16,128]{2,1,0:T(8,128)} %xi_hbm.1, s32[1,16,16]{2,1,0:T(8,128)} %yi_hbm.1, s32[1,16,128]{2,1,0:T(8,128)} %zi_hbm.1, f32[1,3,16,31]{3,2,1,0:T(8,128)} %prof_hbm.1), custom_call_target="tpu_custom_call" | custom-call | tf_op jit(solution)/shard_map/pallas_call | solution.py:339
  24.1 0.7 %copy.8 = f32[16,16,128]{2,1,0:T(8,128)} copy(f32[16,16,128]{2,1,0:T(8,128)S(1)} %shard_map.64) | data formatting | bytes 262144

commit v4 on v3

--- a/solution.py
+++ b/solution.py
@@ -9,7 +9,7 @@
 
 MESH = pl.DeviceIdType.MESH
 ROWS = 8
-GROUP = 8
+GROUP = ROWS
 
 
 def total_of(terms):
@@ -34,19 +34,22 @@
         self.buffer, self.axis, self.count, self.width = buffer, axis, count, width
         self.plane_pieces, self.row_pieces, self.rows = plane_pieces, row_pieces, rows
         self.send, self.recv = sems
+        self.waited = set()
         here = lax.axis_index(axis)
         self.has = (here > 0, here < size - 1)
         self.to = (lax.max(here - 1, 0), lax.min(here + 1, size - 1))
 
-    def copy(self, way, piece, row_piece):
+    def planes(self, way, piece):
         length = self.count // self.plane_pieces
         low, high = piece * length, (piece + 1) * length
         if way == 0:
             high = min(high, self.width)
-            landing = self.count + self.width + low
-        else:
-            low = max(low, self.count - self.width)
-            landing = low - (self.count - self.width)
+            return low, high, self.count + self.width + low
+        low = max(low, self.count - self.width)
+        return low, high, low - (self.count - self.width)
+
+    def copy(self, way, piece, row_piece):
+        low, high, landing = self.planes(way, piece)
         depth = self.rows // self.row_pieces
         rows = pl.ds(row_piece * depth, depth)
         slot = (way * self.plane_pieces + piece) * self.row_pieces + row_piece
@@ -65,11 +68,20 @@
             def _():
                 self.copy(way, piece, row_piece).start()
 
-    def arrive(self, piece, row_piece):
-        for way in (0, 1):
-            @pl.when(self.has[1 - way])
-            def _():
-                self.copy(way, piece, row_piece).wait_recv()
+    def need(self, first, last, row_piece):
+        for way in (0, 1):
+            fresh = []
+            for piece in range(self.plane_pieces):
+                low, high, landing = self.planes(way, piece)
+                spot = (way, piece, row_piece)
+                if landing < last and landing + high - low > first and spot not in self.waited:
+                    self.waited.add(spot)
+                    fresh.append(piece)
+            if fresh:
+                @pl.when(self.has[1 - way])
+                def _():
+                    for piece in fresh:
+                        self.copy(way, piece, row_piece).wait_recv()
 
     def finish(self):
         for way in (0, 1):
@@ -102,15 +114,13 @@
         pltpu.make_async_copy(source, target, in_sems.at[i])
         for i, (source, target) in enumerate(zip(sources, (est, prof, xi, yi, zi, rec)))
     ]
-    for fetch in fetches:
-        fetch.start()
     fetch_est, *fetch_taps, fetch_rec = fetches
     nz, nx, ny = est.shape
     directions, profs, taps = prof.shape[1:]
     half = taps // 2
     zparts, xparts = nz // ROWS, nx // ROWS
     z_halo = Halo(zbuf, "slab", slabs, nz, half, zparts, xparts, nx, (z_send, z_recv))
-    r_halo = Halo(rbuf, "slab", slabs, nz, half, 1, xparts, nx, (r_send, r_recv))
+    r_halo = Halo(rbuf, "slab", slabs, nz, half, zparts, xparts, nx, (r_send, r_recv))
     g_halo = Halo(gbuf, "tile", tiles, nx, half, xparts, zparts, nz, (g_send, g_recv))
     view = lax.axis_index("view")
 
@@ -128,6 +138,8 @@
             barrier, inc=1, device_id={"view": lax.rem(view + step, views)}, device_id_type=MESH
         )
 
+    for fetch in fetch_taps:
+        fetch.start()
     pl.semaphore_wait(barrier, heard)
     e_copy = functools.partial(estimate_copy, g_halo, est_hbm, eland, (e_send, e_recv))
     for zp in range(zparts):
@@ -135,6 +147,9 @@
             @pl.when(g_halo.has[way])
             def _():
                 e_copy(way, zp).start()
+
+    fetch_est.start()
+    fetch_rec.start()
 
     for halo in (z_halo, r_halo, g_halo):
         halo.clear_ends()
@@ -194,12 +209,6 @@
             index = jnp.broadcast_to(lines[:, x : x + 1], (ROWS, ny)) + profs
             for k in range(taps):
                 wy[k, x, rows, :] = jnp.where(inside[k], tap(k, index), 0.0)
-    for xp in range(xparts):
-        rows = pl.ds(xp * ROWS, ROWS)
-        index = zi[0, rows, :] + 2 * profs
-        for k in range(taps):
-            wz[k, rows, :] = tap(k, index)
-
     def blur(field, weights, first, rows, adjoint):
         taps_here = [weights[k, rows, :] for k in range(taps)]
         reads = [field[first + i, rows, :] for i in range(GROUP + taps - 1)]
@@ -230,46 +239,38 @@
             def _():
                 ebuf[at : at + half, rows, :] = jnp.zeros((half, ROWS, ny), ebuf.dtype)
 
-        def forward(g, carry):
-            first = g * GROUP
+        for xp in range(xparts):
+            first = xp * GROUP
             for i, line in enumerate(blur(ebuf, wx, first, rows, False)):
                 spot = (half + zp * ROWS) * nx + first + i
                 flat_z[pl.ds(spot, ROWS, stride=nx), :] = y_forward(line, first + i, rows)
-            return carry
-
-        lax.fori_loop(0, nx // GROUP, forward, 0)
-        for xp in range(xparts):
             z_halo.start(zp, xp)
 
     for xp in range(xparts):
+        rows = pl.ds(xp * ROWS, ROWS)
+        index = zi[0, rows, :] + 2 * profs
+        for k in range(taps):
+            wz[k, rows, :] = tap(k, index)
+
+    reach = GROUP + taps - 1
+    for xp in range(xparts):
+        rows = pl.ds(xp * ROWS, ROWS)
         for zp in range(zparts):
-            z_halo.arrive(zp, xp)
-        rows = pl.ds(xp * ROWS, ROWS)
-
-        def divide(g, carry):
-            first = g * GROUP
+            first = zp * GROUP
+            z_halo.need(first, first + reach, xp)
             for i, blurred in enumerate(blur(zbuf, wz, first, rows, False)):
                 rbuf[half + first + i, rows, :] = rec[0, first + i, rows, :] / blurred
-            return carry
-
-        lax.fori_loop(0, nz // GROUP, divide, 0)
-        r_halo.start(0, xp)
+            r_halo.start(zp, xp)
 
     flat_t = tbuf.reshape(nz * nx, ny)
     for zp in range(zparts):
         z_rows = pl.ds(zp * ROWS, ROWS)
         for xp in range(xparts):
             rows = pl.ds(xp * ROWS, ROWS)
-
-            def back_z(g, carry):
-                first = g * GROUP
-                for i, line in enumerate(blur(rbuf, wz, first, rows, True)):
-                    tbuf[first + i, rows, :] = line
-                return carry
-
-            if zp == 0:
-                r_halo.arrive(0, xp)
-                lax.fori_loop(0, nz // GROUP, back_z, 0)
+            first = zp * GROUP
+            r_halo.need(first, first + reach, xp)
+            for i, line in enumerate(blur(rbuf, wz, first, rows, True)):
+                tbuf[first + i, rows, :] = line
 
             def back_y(i, carry):
                 x = xp * ROWS + i
@@ -280,9 +281,9 @@
             lax.fori_loop(0, ROWS, back_y, 0, unroll=4)
             g_halo.start(xp, zp)
 
-    def view_copy(step, zp):
-        piece = vbuf.at[view, pl.ds(zp * ROWS, ROWS)]
-        slot = (step - 1) * zparts + zp
+    def view_copy(step, zp, xp):
+        piece = vbuf.at[view, pl.ds(zp * ROWS, ROWS), pl.ds(xp * ROWS, ROWS)]
+        slot = ((step - 1) * zparts + zp) * xparts + xp
         return pltpu.make_async_remote_copy(
             src_ref=piece, dst_ref=piece, send_sem=v_send.at[slot], recv_sem=v_recv.at[slot],
             device_id={"view": lax.rem(view + step, views)}, device_id_type=MESH,
@@ -290,25 +291,14 @@
 
     flat_v = vbuf.reshape(views * nz * nx, ny)
     for zp in range(zparts):
-        for xp in range(xparts):
-            g_halo.arrive(xp, zp)
         rows = pl.ds(zp * ROWS, ROWS)
-
-        def back_x(g, carry):
-            first = g * GROUP
+        for xp in range(xparts):
+            first = xp * GROUP
+            g_halo.need(first, first + reach, zp)
             for i, line in enumerate(blur(gbuf, wx, first, rows, True)):
                 flat_v[pl.ds((view * nz + zp * ROWS) * nx + first + i, ROWS, stride=nx), :] = line
-            return carry
-
-        lax.fori_loop(0, nx // GROUP, back_x, 0)
-        for step in range(1, views):
-            view_copy(step, zp).start()
-
-    for zp in range(zparts):
-        for step in range(1, views):
-            view_copy(step, zp).wait_recv()
-        planes = pl.ds(zp * ROWS, ROWS)
-        out[planes] = est[planes] * total_of(vbuf[v, planes] for v in range(views)) / views
+            for step in range(1, views):
+                view_copy(step, zp, xp).start()
 
     for halo in (z_halo, r_halo, g_halo):
         halo.finish()
@@ -318,8 +308,17 @@
             for zp in range(zparts):
                 e_copy(way, zp).wait_send()
     for zp in range(zparts):
-        for step in range(1, views):
-            view_copy(step, zp).wait_send()
+        planes = pl.ds(zp * ROWS, ROWS)
+        for xp in range(xparts):
+            rows = pl.ds(xp * ROWS, ROWS)
+            for step in range(1, views):
+                view_copy(step, zp, xp).wait_recv()
+            total = total_of(vbuf[v, planes, rows] for v in range(views))
+            out[planes, rows] = est[planes, rows] * total / views
+    for zp in range(zparts):
+        for xp in range(xparts):
+            for step in range(1, views):
+                view_copy(step, zp, xp).wait_send()
 
 
 def shards(sizes, *args):
@@ -333,9 +332,9 @@
     assert directions * profs <= 128
     zparts, xparts = nz // ROWS, nx // ROWS
     f32 = jnp.float32
-    counts = (zparts, zparts * xparts, xparts, zparts * xparts)
+    counts = (zparts, *[zparts * xparts] * 3)
     sems = [pltpu.SemaphoreType.DMA((2 * c,)) for c in counts for _ in range(2)]
-    sems += [pltpu.SemaphoreType.DMA((max(1, views - 1) * zparts,)) for _ in range(2)]
+    sems += [pltpu.SemaphoreType.DMA((max(1, views - 1) * zparts * xparts,)) for _ in range(2)]
     return pl.pallas_call(
         functools.partial(kernel, sizes),
         out_shape=jax.ShapeDtypeStruct(estimate.shape, f32),

time: 24.9 us -> 23.1 us (0.928)
  Pallas kernels: 24.1 us -> 22.3 us
    pallas_call x1, Pallas kernels: 24.1 us -> 22.3 us  [shards(): pl.pallas_call(functools.partial(kernel, sizes), out_shape=jax.ShapeDtype...]
where the time goes in v4:
time: 23.1 us; the launch traced here: 23 us
  Pallas kernels  22.3 us (97%)
  local copies, waits for them, and re-layouts  0.66 us (3%)
    pallas_call x1, Pallas kernels, shards(): pl.pallas_call(functools.partial(kernel, sizes), out_shape=jax.ShapeDtype...  22.3 us
    unnamed x1, local copies, waits for them, and re-layouts  0.66 us

profile of v4, /device:TPU:0, one launch (start us, length us, event | category | flops | bytes accessed | tf_op | source)
XLA Modules:
  0.0 23.0 jit_solution(13016092452254560541)
XLA Ops:
  0.0 22.3 %shard_map.64 = f32[16,16,128]{2,1,0:T(8,128)S(1)} custom-call(f32[16,16,128]{2,1,0:T(8,128)} %est_hbm.1, f32[1,16,16,128]{3,2,1,0:T(8,128)} %rec_hbm.1, s32[1,16,128]{2,1,0:T(8,128)} %xi_hbm.1, s32[1,16,16]{2,1,0:T(8,128)} %yi_hbm.1, s32[1,16,128]{2,1,0:T(8,128)} %zi_hbm.1, f32[1,3,16,31]{3,2,1,0:T(8,128)} %prof_hbm.1), custom_call_target="tpu_custom_call" | custom-call | tf_op jit(solution)/shard_map/pallas_call | solution.py:338
  22.3 0.7 %copy.8 = f32[16,16,128]{2,1,0:T(8,128)} copy(f32[16,16,128]{2,1,0:T(8,128)S(1)} %shard_map.64) | data formatting | bytes 262144

commit v5 on v4

--- a/solution.py
+++ b/solution.py
@@ -210,12 +210,16 @@
             for k in range(taps):
                 wy[k, x, rows, :] = jnp.where(inside[k], tap(k, index), 0.0)
     def blur(field, weights, first, rows, adjoint):
-        taps_here = [weights[k, rows, :] for k in range(taps)]
-        reads = [field[first + i, rows, :] for i in range(GROUP + taps - 1)]
-        return [
-            total_of(taps_here[k] * reads[i + (taps - 1 - k if adjoint else k)] for k in range(taps))
-            for i in range(GROUP)
-        ]
+        totals, loaded = [None] * GROUP, {}
+        for j in range(GROUP + taps - 1):
+            read = field[first + j, rows, :]
+            for i in range(max(0, j - taps + 1), min(GROUP, j + 1)):
+                k = taps - 1 - (j - i) if adjoint else j - i
+                if k not in loaded:
+                    loaded[k] = weights[k, rows, :]
+                term = loaded[k] * read
+                totals[i] = term if totals[i] is None else totals[i] + term
+        return totals
 
     def turn(source, planes, zp, first, at):
         for i in range(planes):
@@ -272,13 +276,9 @@
             for i, line in enumerate(blur(rbuf, wz, first, rows, True)):
                 tbuf[first + i, rows, :] = line
 
-            def back_y(i, carry):
-                x = xp * ROWS + i
+            for x in range(xp * ROWS, (xp + 1) * ROWS):
                 line = flat_t[pl.ds(zp * ROWS * nx + x, ROWS, stride=nx), :]
                 gbuf[half + x, z_rows, :] = y_back(line, x, z_rows)
-                return carry
-
-            lax.fori_loop(0, ROWS, back_y, 0, unroll=4)
             g_halo.start(xp, zp)
 
     def view_copy(step, zp, xp):

time: 23.1 us -> 23 us (level)
  no operation moved by 1% of the time
where the time goes in v5:
time: 23 us; the launch traced here: 22.8 us
  Pallas kernels  22.2 us (97%)
  local copies, waits for them, and re-layouts  0.66 us (3%)
    pallas_call x1, Pallas kernels, shards(): pl.pallas_call(functools.partial(kernel, sizes), out_shape=jax.ShapeDtype...  22.2 us
    unnamed x1, local copies, waits for them, and re-layouts  0.66 us

profile of v5, /device:TPU:0, one launch (start us, length us, event | category | flops | bytes accessed | tf_op | source)
XLA Modules:
  0.0 22.8 jit_solution(15792610240024449704)
XLA Ops:
  0.0 22.2 %shard_map.64 = f32[16,16,128]{2,1,0:T(8,128)S(1)} custom-call(f32[16,16,128]{2,1,0:T(8,128)} %est_hbm.1, f32[1,16,16,128]{3,2,1,0:T(8,128)} %rec_hbm.1, s32[1,16,128]{2,1,0:T(8,128)} %xi_hbm.1, s32[1,16,16]{2,1,0:T(8,128)} %yi_hbm.1, s32[1,16,128]{2,1,0:T(8,128)} %zi_hbm.1, f32[1,3,16,31]{3,2,1,0:T(8,128)} %prof_hbm.1), custom_call_target="tpu_custom_call" | custom-call | tf_op jit(solution)/shard_map/pallas_call | solution.py:338
  22.2 0.7 %copy.8 = f32[16,16,128]{2,1,0:T(8,128)} copy(f32[16,16,128]{2,1,0:T(8,128)S(1)} %shard_map.64) | data formatting | bytes 262144
